TPU v7x, 32 devices: a whole 2x2x4 slice. The times are simulated.
32 devices in a mesh: shard: 8 (over z, y), tensor: 4 (over x, core).
Axes of the slice: x: 2, y: 2, z: 4, core: 2. Of those that a mesh axis runs over, the one named last changes fastest.
Arguments:
- grad_parts: float32 [4, 4, 768, 768], P('tensor', None, 'shard'), may hold values from -0.6 to 0.6
- adam_v: float32 [4, 768, 768], P(None, 'shard', 'tensor'), may hold values from 0.01 to 0.2
- left_stat: float32 [8, 768, 768], P('shard', 'tensor'), may hold values from -6 to 6
- right_stat: float32 [8, 768, 768], P('shard', 'tensor'), may hold values from -6 to 6
- left_root: bfloat16 [8, 768, 768], P('shard', 'tensor'), as said below
- right_root: bfloat16 [8, 768, 768], P('shard', 'tensor'), as said below
- owner: int32 [4], replicated, may hold values from 0 to 7, as said below
- vec_parts: float32 [4, 4, 768], P('tensor', None, 'shard'), may hold values from -0.6 to 0.6
- vec_m: float32 [4, 768], P(None, 'shard'), may hold values from -0.3 to 0.3
- vec_v: float32 [4, 768], P(None, 'shard'), may hold values from 0.01 to 0.2
Outputs:
- update: float32 [4, 768, 768], P(None, 'shard', 'tensor')
- new_adam_v: float32 [4, 768, 768], P(None, 'shard', 'tensor')
- new_left: float32 [8, 768, 768], P('shard', 'tensor')
- new_right: float32 [8, 768, 768], P('shard', 'tensor')
- new_vec_m: float32 [4, 768], P(None, 'shard')
- new_vec_v: float32 [4, 768], P(None, 'shard')
- vec_step: float32 [4, 768], P(None, 'shard')
Inputs may be any that keep to these rules, and one draw needn't show every extreme that they name: owner holds 4 distinct slot numbers: no slot owns two tiles. `left_root`: each slot's matrix is symmetric. `right_root`: each slot's matrix is symmetric.
All inputs are finite; a program needn't handle non-finite values.
Results may differ from a plain program's by a relative error of at most 0.0003.
Values may be sent and summed in bfloat16 or wider, within the bound.
No kernel may reach another device: no remote copies, remote signals or barrier semaphores. Data moves between devices by JAX's collectives and lax.ppermute only.
A program may use at most 64 MiB of HBM per device.

v0:
```python
import jax
import jax.numpy as jnp
from jax import lax
from jax.sharding import PartitionSpec as P

BETA_ONE = 0.9
BETA_TWO = 0.95
STAT_DECAY = 0.95
STEP_COUNT = 10.0
EPSILON = 1e-08
NORM_EPS = 1e-06
HIGH = lax.Precision.HIGHEST


def local(
    grad_parts, adam_v, left_stat, right_stat, left_root, right_root, owner, vec_parts, vec_m, vec_v
):
    shards = lax.axis_size("shard")
    tiles = owner.shape[0]
    grad = lax.psum_scatter(grad_parts[0], "tensor", scatter_dimension=2, tiled=True)
    rows_dev = grad.shape[1]
    cols_dev = grad.shape[2]
    new_adam_v = BETA_TWO * adam_v + (1.0 - BETA_TWO) * grad * grad
    bias_two = 1.0 - BETA_TWO**STEP_COUNT
    adam_dir = grad / (jnp.sqrt(new_adam_v / bias_two) + EPSILON)
    adam_sq = jnp.sum(adam_dir * adam_dir, axis=(1, 2))
    vec_grad = lax.psum(vec_parts[0], "tensor")
    new_vec_m = BETA_ONE * vec_m + (1.0 - BETA_ONE) * vec_grad
    new_vec_v = BETA_TWO * vec_v + (1.0 - BETA_TWO) * vec_grad * vec_grad
    bias_one = 1.0 - BETA_ONE**STEP_COUNT
    vec_step = new_vec_m / bias_one / (jnp.sqrt(new_vec_v / bias_two) + EPSILON)
    slot_hot = (jnp.arange(shards, dtype=jnp.int32)[:, None] == owner[None, :]).astype(jnp.float32)
    outgoing = jnp.dot(slot_hot, grad.reshape(tiles, rows_dev * cols_dev), precision=HIGH)
    outgoing = outgoing.reshape(shards, rows_dev, cols_dev)
    arrived = lax.all_to_all(outgoing, "shard", split_axis=0, concat_axis=1, tiled=True)[0]
    whole = lax.all_gather(arrived, "tensor", axis=1, tiled=True)
    start = lax.axis_index("tensor") * cols_dev
    tile_rows = lax.dynamic_slice_in_dim(whole, start, cols_dev, 0)
    new_left = STAT_DECAY * left_stat[0] + (1.0 - STAT_DECAY) * jnp.dot(
        tile_rows, whole.T, precision=HIGH
    )
    new_right = STAT_DECAY * right_stat[0] + (1.0 - STAT_DECAY) * jnp.dot(
        arrived.T, whole, precision=HIGH
    )
    right_full = lax.all_gather(right_root[0], "tensor", axis=0, tiled=True).astype(jnp.float32)
    left_part = jnp.dot(left_root[0].astype(jnp.float32), whole, precision=HIGH)
    row_block = jnp.dot(left_part, right_full, precision=HIGH)
    direction = lax.all_to_all(row_block[None], "tensor", split_axis=2, concat_axis=1, tiled=True)[
        0
    ]
    returned = lax.all_to_all(
        direction.reshape(shards, rows_dev, cols_dev),
        "shard",
        split_axis=0,
        concat_axis=0,
        tiled=True,
    )
    update = jnp.dot(slot_hot.T, returned.reshape(shards, rows_dev * cols_dev), precision=HIGH)
    update = update.reshape(tiles, rows_dev, cols_dev)
    shampoo_local = jnp.sum(update * update, axis=(1, 2))
    adam_total, shampoo_total = lax.psum((adam_sq, shampoo_local), ("shard", "tensor"))
    graft = jnp.sqrt(adam_total) / (jnp.sqrt(shampoo_total) + NORM_EPS)
    update = graft[:, None, None] * update
    return (update, new_adam_v, new_left[None], new_right[None], new_vec_m, new_vec_v, vec_step)


def solution(mesh):
    in_specs = (
        P("tensor", None, "shard", None),
        P(None, "shard", "tensor"),
        P("shard", "tensor", None),
        P("shard", "tensor", None),
        P("shard", "tensor", None),
        P("shard", "tensor", None),
        P(),
        P("tensor", None, "shard"),
        P(None, "shard"),
        P(None, "shard"),
    )
    out_specs = (
        P(None, "shard", "tensor"),
        P(None, "shard", "tensor"),
        P("shard", "tensor", None),
        P("shard", "tensor", None),
        P(None, "shard"),
        P(None, "shard"),
        P(None, "shard"),
    )
    return jax.shard_map(local, mesh=mesh, in_specs=in_specs, out_specs=out_specs, check_vma=False)
```

profile of v0, /device:TPU:0, one launch (start us, length us, event | category | flops | bytes accessed | tf_op | source)
XLA Modules:
  0.0 205.5 jit_solution(14201237901707531373)
XLA Ops:
  7.2 0.0 copy-start
  7.2 0.0 reduce-scatter.4.cloned.1.call-start
  7.2 1.8 copy.38
  9.0 1.8 reshape.39
  10.8 0.0 copy-start.4
  10.8 0.0 reduce-scatter.4.cloned.1.call-update
  10.8 0.0 all-gather.4.cloned.1.call-start
  10.9 28.5 %reduce-scatter.4.cloned.1.call-done = f32[192,384]{1,0:T(8,128)} async-done(((f32[768,384]{1,0:T(8,128)}), f32[192,384]{1,0:T(8,128)}) %reduce-scatter.4.cloned.1.call-update) | async-done | bytes 294928
  39.4 1.2 reshape.40
  40.6 0.2 copy.39
  40.9 0.0 copy-start.2
  40.9 0.2 reshape.35
  41.1 0.2 dot_general.27
  41.3 0.0 copy-done.4
  41.4 0.8 fusion.9
  42.2 0.0 copy-done.2
  42.2 0.3 copy.30
  42.4 25.5 %all_to_all.29 = f32[8,96,192]{2,1,0:T(8,128)S(1)} all-to-all(f32[8,96,192]{2,1,0:T(8,128)S(1)} %copy.30), channel_id=1, replica_groups=mesh['shard'=8,'tensor'=4] {'shard'}, dimensions={0} | all-to-all | bytes 1179648 | tf_op jit(solution)/shard_map/all_to_all | solution.py:35
  67.9 1.1 copy.37
  69.0 0.0 all-gather.4.cloned.1.call-update
  69.0 0.0 all-gather.6.cloned.1.call-start
  69.1 0.7 all-gather.6.cloned.1.call-update
  69.7 21.6 %all-gather.4.cloned.1.call-done = f32[768,768]{0,1:T(8,128)} async-done(((f32[768,192]{0,1:T(8,128)}), f32[768,768]{0,1:T(8,128)}) %all-gather.4.cloned.1.call-update) | async-done | bytes 2359312 | tf_op jit(solution)/shard_map/all_gather | solution.py:36
  91.3 0.0 copy-done
  91.3 3.1 %fusion.11 = f32[768,192]{0,1:T(8,128)S(1)} fusion(f32[768,768]{0,1:T(8,128)} %all-gather.4.cloned.1.call-done, bf16[1,192,768]{2,1,0:T(8,128)(2,1)S(1)} %copy-done), kind=kOutput, calls=%fused_computation.17 | convolution fusion | flops 1358954496 | bytes 3244032 | tf_op jit(solution)/shard_map/dot_general | solution.py:46
  94.4 16.0 %all-gather.6.cloned.1.call-done = bf16[1,768,768]{2,1,0:T(8,128)(2,1)} async-done(((bf16[1,192,768]{2,1,0:T(8,128)(2,1)}), bf16[1,768,768]{2,1,0:T(8,128)(2,1)}) %all-gather.6.cloned.1.call-update) | async-done | bytes 1179664 | tf_op jit(solution)/shard_map/all_gather | solution.py:45
  110.4 2.1 %convolution_bitcast_fusion = f32[1,192,768]{2,1,0:T(8,128)S(1)} fusion(f32[768,192]{0,1:T(8,128)S(1)} %fusion.11, bf16[1,768,768]{2,1,0:T(8,128)(2,1)} %all-gather.6.cloned.1.call-done), kind=kOutput, calls=%fused_computation.6 | convolution fusion | flops 1358954496 | bytes 2359296 | tf_op jit(solution)/shard_map/dot_general | solution.py:47
  112.6 0.6 copy.32
  113.2 14.1 %all_to_all.30 = f32[1,192,768]{1,0,2:T(1,128)S(1)} all-to-all(f32[1,192,768]{1,0,2:T(1,128)S(1)} %copy.32), channel_id=1, replica_groups=mesh['shard'=8,'tensor'=4] {'tensor'}, dimensions={2} | all-to-all | bytes 1179648 | tf_op jit(solution)/shard_map/all_to_all | solution.py:48
  127.2 0.4 copy.33
  127.7 0.0 copy-start.5
  127.7 0.0 copy-start.6
  127.7 0.0 copy-start.7
  127.7 1.5 all_to_all.23
  129.2 0.0 copy-start.1
  129.2 2.3 %copy.34 = f32[1,4,192,192]{3,2,1,0:T(8,128)} copy(f32[1,4,192,192]{3,1,2,0:T(4,128)} %bitcast.44) | data formatting | bytes 1179648 | tf_op jit(solution)/shard_map/all_to_all | solution.py:48
  131.5 5.5 %all-to-all-start.2 = ((f32[8,96,192]{2,1,0:T(8,128)}), f32[8,96,192]{2,1,0:T(8,128)}, u32[]{:S(2)}, u32[]{:S(2)}) async-start(f32[8,96,192]{2,1,0:T(8,128)} %bitcast.43), calls=%async_computation.2 | async-start | bytes 1572864 | tf_op jit(solution)/shard_map/all_to_all | solution.py:51
  137.0 0.0 copy-done.5
  137.0 6.2 %psum.23 = f32[4,96]{1,0:T(4,128)S(1)} all-reduce(f32[4,96]{1,0:T(4,128)S(1)} %bitcast.49), channel_id=1, replica_groups=mesh['shard'=8,'tensor'=4] {'tensor'}, use_global_device_ids=true, to_apply=%region_5.0 | all-reduce | flops 384 | bytes 3072 | tf_op jit(solution)/shard_map/psum | solution.py:27
  143.3 0.0 copy-done.6
  143.3 0.0 copy-done.7
  143.3 0.6 add_divide_fusion
  143.9 0.0 copy-start.3
  143.9 2.1 %multiply_reduce_fusion.1 = (f32[4]{0:T(128)S(1)}, f32[4,96,192]{2,1,0:T(8,128)}) fusion(f32[4,96,192]{2,1,0:T(8,128)} %copy-done.2, f32[4,96,192]{2,1,0:T(8,128)} %param.11), kind=kLoop, calls=%fused_computation.16 | loop fusion | flops 663548 | bytes 884752 | tf_op jit(solution)/shard_map/reduce_sum | solution.py:26
  146.0 0.0 copy-done.1
  146.0 4.0 %fusion.3 = f32[1,192,768]{2,1,0:T(8,128)} fusion(f32[768,768]{0,1:T(8,128)S(1)} %copy-done.1, s32[]{:T(128)S(6)} %select_n.3, f32[1,192,768]{2,1,0:T(8,128)} %param.12), kind=kOutput, calls=%fused_computation.5 | convolution fusion | flops 1359396864 | bytes 4325380 | tf_op jit(solution)/shard_map/dot_general | solution.py:39
  150.0 0.0 copy-done.3
  150.0 4.8 %fusion.1 = f32[1,192,768]{2,1,0:T(8,128)} fusion(f32[768,192]{1,0:T(8,128)S(1)} %bitcast.41, f32[768,768]{0,1:T(8,128)S(1)} %copy-done.1, f32[1,192,768]{2,1,0:T(8,128)S(1)} %copy-done.3), kind=kOutput, calls=%fused_computation.2 | convolution fusion | flops 1359396864 | bytes 4128768 | tf_op jit(solution)/shard_map/dot_general | solution.py:42
  154.8 2.2 %all-to-all-done.2 = f32[8,96,192]{2,1,0:T(8,128)} async-done(((f32[8,96,192]{2,1,0:T(8,128)}), f32[8,96,192]{2,1,0:T(8,128)}, u32[]{:S(2)}, u32[]{:S(2)}) %all-to-all-start.2) | async-done | bytes 589856 | tf_op jit(solution)/shard_map/all_to_all | solution.py:51
  157.0 1.4 reshape.36
  158.5 0.3 dot_general.32
  158.8 1.1 multiply_reduce_fusion
  159.9 38.0 %all-reduce = (f32[4]{0:T(128)S(1)}, f32[4]{0:T(128)S(1)}) all-reduce(f32[4]{0:T(128)S(1)} %get-tuple-element.42, f32[4]{0:T(128)S(1)} %get-tuple-element.40), channel_id=1, replica_groups=mesh['shard'=8,'tensor'=4] {'shard','tensor'}, use_global_device_ids=true, to_apply=%region_4.0 | all-reduce | flops 8 | bytes 64 | tf_op jit(solution)/shard_map/psum | solution.py:61
  198.0 0.1 broadcast_multiply_fusion
  198.1 0.8 copy.36
  (1 shorter events, 0.0 us)
Async XLA Ops:
  7.2 84.1 %copy-start = (bf16[1,192,768]{2,1,0:T(8,128)(2,1)S(1)}, bf16[1,192,768]{2,1,0:T(8,128)(2,1)}, u32[]{:S(2)}) copy-start(bf16[1,192,768]{2,1,0:T(8,128)(2,1)} %param.14) | copy-start | bytes 884740
  7.2 32.2 %reduce-scatter.4.cloned.1.call-start = ((), (), s32[]{:S(2)}) async-start(), calls=%async_computation.6 | async-start | bytes 1474560
  10.8 30.5 %copy-start.4 = (s32[4]{0:T(128)S(1)}, s32[4]{0:T(128)}, u32[]{:S(2)}) copy-start(s32[4]{0:T(128)} %param.16) | copy-start | bytes 52
  10.8 80.5 %all-gather.4.cloned.1.call-start = ((), (), s32[]{:S(2)}) async-start(), calls=%async_computation.4 | async-start | bytes 2949120 | tf_op jit(solution)/shard_map/all_gather | solution.py:36
  40.9 1.3 copy-start.2
  69.0 41.4 %all-gather.6.cloned.1.call-start = ((), (), s32[]{:S(2)}) async-start(), calls=%async_computation.5 | async-start | bytes 1474560 | tf_op jit(solution)/shard_map/all_gather | solution.py:45
  127.7 9.3 %copy-start.5 = (f32[1,4,96]{2,1,0:T(4,128)S(1)}, f32[1,4,96]{2,1,0:T(4,128)}, u32[]{:S(2)}) copy-start(f32[1,4,96]{2,1,0:T(4,128)} %param.17) | copy-start | bytes 4612
  127.7 15.6 %copy-start.6 = (f32[4,96]{1,0:T(4,128)S(1)}, f32[4,96]{1,0:T(4,128)}, u32[]{:S(2)}) copy-start(f32[4,96]{1,0:T(4,128)} %param.19) | copy-start | bytes 4612
  127.7 15.6 %copy-start.7 = (f32[4,96]{1,0:T(4,128)S(1)}, f32[4,96]{1,0:T(4,128)}, u32[]{:S(2)}) copy-start(f32[4,96]{1,0:T(4,128)} %param.18) | copy-start | bytes 4612
  129.2 16.8 %copy-start.1 = (f32[768,768]{0,1:T(8,128)S(1)}, f32[768,768]{0,1:T(8,128)}, u32[]{:S(2)}) copy-start(f32[768,768]{0,1:T(8,128)} %all-gather.4.cloned.1.call-done) | copy-start | bytes 7077892
  131.5 25.5 %all-to-all-start.2 = ((f32[8,96,192]{2,1,0:T(8,128)}), f32[8,96,192]{2,1,0:T(8,128)}, u32[]{:S(2)}, u32[]{:S(2)}) async-start(f32[8,96,192]{2,1,0:T(8,128)} %bitcast.43), calls=%async_computation.2 | async-start | bytes 1572864 | tf_op jit(solution)/shard_map/all_to_all | solution.py:51
  143.9 6.1 %copy-start.3 = (f32[1,192,768]{2,1,0:T(8,128)S(1)}, f32[1,192,768]{2,1,0:T(8,128)}, u32[]{:S(2)}) copy-start(f32[1,192,768]{2,1,0:T(8,128)} %param.13) | copy-start | bytes 1769476
Sparse Core Ops, SparseCore 0:
  11.0 28.4 reduce-scatter.3
  69.1 22.1 all-gather.3
  93.0 17.4 all-gather.5
where the time goes:
time: 206 us; the launch traced here: 205 us
  blocking collectives  83.8 us (41%)
  waiting for transfers between devices  69.1 us (34%)
  matrix products  16 us (8%)
  local copies, waits for them, and re-layouts  14.2 us (7%)
  between operations  13.9 us (7%)
  starting transfers between devices  5.64 us (3%)
  other arithmetic  2.89 us (1%)
    psum x1, blocking collectives, local(): lax.psum((adam_sq, shampoo_local), ('shard', 'tensor'))  38 us
    unnamed x4, waiting for transfers between devices  29.3 us
    all_to_all x1, blocking collectives, local(): lax.all_to_all(outgoing, 'shard', split_axis=0, concat_axis=1, tiled=True)  25.5 us
    all_gather x1, waiting for transfers between devices, local(): whole = lax.all_gather(arrived, 'tensor', axis=1, tiled=True)  21.6 us
    all_gather x1, waiting for transfers between devices, local(): lax.all_gather(right_root[0], 'tensor', axis=0, tiled=True)  16 us
    all_to_all x1, blocking collectives, local(): lax.all_to_all(row_block[None], 'tensor', split_axis=2, concat_axis=1, ti...  14.1 us
    psum x1, blocking collectives, local(): vec_grad = lax.psum(vec_parts[0], 'tensor')  6.25 us
    unnamed x21, local copies, waits for them, and re-layouts  5.86 us
  transfers between devices with their start and end apart: 4, of which 4 were waited for; matrix products, arithmetic and copies ran while one was open for 7% of the time, Pallas kernels for 0%

commit v1 on v0

--- a/solution.py
+++ b/solution.py
@@ -10,6 +10,28 @@
 EPSILON = 1e-08
 NORM_EPS = 1e-06
 HIGH = lax.Precision.HIGHEST
+
+
+def joined_along(tiles, dim):
+    tiles = jnp.moveaxis(tiles, 0, dim)
+    shape = tiles.shape
+    return tiles.reshape(*shape[:dim], shape[dim] * shape[dim + 1], *shape[dim + 2 :])
+
+
+def collect(x, axis, dim):
+    size = lax.axis_size(axis)
+    pairs = [(i, (i + 1) % size) for i in range(size)]
+    back = [(b, a) for a, b in pairs]
+    lower, upper = ([], [])
+    for step in range(size - 1):
+        if step % 2 == 0:
+            lower.append(lax.ppermute(lower[-1] if lower else x, axis, pairs))
+        else:
+            upper.append(lax.ppermute(upper[-1] if upper else x, axis, back))
+    tiles = jnp.stack([*lower[::-1], x, *upper])
+    shift = lax.axis_index(axis) - len(lower)
+    tiles = tiles[(jnp.arange(size) - shift) % size]
+    return joined_along(tiles, dim)
 
 
 def local(
@@ -42,7 +64,7 @@
     new_right = STAT_DECAY * right_stat[0] + (1.0 - STAT_DECAY) * jnp.dot(
         arrived.T, whole, precision=HIGH
     )
-    right_full = lax.all_gather(right_root[0], "tensor", axis=0, tiled=True).astype(jnp.float32)
+    right_full = collect(right_root[0], "tensor", 0).astype(jnp.float32)
     left_part = jnp.dot(left_root[0].astype(jnp.float32), whole, precision=HIGH)
     row_block = jnp.dot(left_part, right_full, precision=HIGH)
     direction = lax.all_to_all(row_block[None], "tensor", split_axis=2, concat_axis=1, tiled=True)[

time: 206 us -> 190 us (0.922)
  waiting for transfers between devices: 69.1 us -> 55 us
    ppermute x0 -> x3, waiting for transfers between devices: none -> 19.4 us  [the longest x2 17.5 us: collect(): lower.append(lax.ppermute(lower[-1] if lower else x, axis, pairs))]
    all_gather x1, waiting for transfers between devices: 21.6 us -> 4.64 us  [local(): whole = lax.all_gather(arrived, 'tensor', axis=1, tiled=True)]
    all_gather x1 -> x0, waiting for transfers between devices: 16 us -> none  [local(): lax.all_gather(right_root[0], 'tensor', axis=0, tiled=True)]
    all_to_all x3, local copies, waits for them, and re-layouts: 4.23 us -> 2.06 us  [local(): lax.all_to_all(row_block[None], 'tensor', split_axis=2, concat_axis=1, ti...]
    unnamed x4 -> x3, waiting for transfers between devices: 29.3 us -> 28.6 us
    unnamed x21 -> x23, local copies, waits for them, and re-layouts: 5.86 us -> 5.85 us
  transfers between devices with their start and end apart: 4 -> 6, of which waited for: 4 -> 6; matrix products, arithmetic and copies ran while one was open for 7% -> 6% of each run, Pallas kernels for 0% -> 0%
where the time goes in v1:
time: 190 us
  blocking collectives  83.8 us (44%)
  waiting for transfers between devices  55 us (29%)
  matrix products  14.8 us (8%)
  between operations  14.2 us (7%)
  local copies, waits for them, and re-layouts  12.7 us (7%)
  starting transfers between devices  6.29 us (3%)
  other arithmetic  2.99 us (2%)
    psum x1, blocking collectives, local(): lax.psum((adam_sq, shampoo_local), ('shard', 'tensor'))  38 us
    unnamed x3, waiting for transfers between devices  28.6 us
    all_to_all x1, blocking collectives, local(): lax.all_to_all(outgoing, 'shard', split_axis=0, concat_axis=1, tiled=True)  25.5 us
    ppermute x2, waiting for transfers between devices, collect(): lower.append(lax.ppermute(lower[-1] if lower else x, axis, pairs))  17.5 us
    all_to_all x1, blocking collectives, local(): lax.all_to_all(row_block[None], 'tensor', split_axis=2, concat_axis=1, ti...  14.1 us
    psum x1, blocking collectives, local(): vec_grad = lax.psum(vec_parts[0], 'tensor')  6.25 us
    unnamed x23, local copies, waits for them, and re-layouts  5.85 us
    dot_general x1, matrix products, local(): jnp.dot(arrived.T, whole, precision=HIGH)  4.77 us
  transfers between devices with their start and end apart: 6, of which 6 were waited for; matrix products, arithmetic and copies ran while one was open for 6% of the time, Pallas kernels for 0%

profile of v1, /device:TPU:0, one launch (start us, length us, event | category | flops | bytes accessed | tf_op | source)
XLA Modules:
  0.0 189.7 jit_solution(6651772876924030108)
XLA Ops:
  7.2 0.0 copy-start
  7.2 0.0 reduce-scatter.4.cloned.1.call-start
  7.2 1.8 copy.38
  9.0 1.8 reshape.99
  10.8 0.0 reduce-scatter.4.cloned.1.call-update
  10.8 0.0 all-gather.2.cloned.1.call-start
  10.9 28.5 %reduce-scatter.4.cloned.1.call-done = f32[192,384]{1,0:T(8,128)} async-done(((f32[768,384]{1,0:T(8,128)}), f32[192,384]{1,0:T(8,128)}) %reduce-scatter.4.cloned.1.call-update) | async-done | bytes 294928
  39.4 1.2 reshape.100
  40.6 0.0 copy-start.5
  40.7 0.2 copy.39
  40.9 0.0 copy-start.2
  40.9 0.2 reshape.87
  41.1 0.2 dot_general.27
  41.3 0.0 copy-done.5
  41.4 0.8 fusion.8
  42.2 0.0 copy-done.2
  42.2 0.3 copy.30
  42.5 25.5 %all_to_all.29 = f32[8,96,192]{2,1,0:T(8,128)S(1)} all-to-all(f32[8,96,192]{2,1,0:T(8,128)S(1)} %copy.30), channel_id=1, replica_groups=mesh['shard'=8,'tensor'=4] {'shard'}, dimensions={0} | all-to-all | bytes 1179648 | tf_op jit(solution)/shard_map/all_to_all | solution.py:57
  67.9 0.0 copy-start.4
  67.9 1.1 copy.37
  69.0 0.0 all-gather.2.cloned.1.call-update
  69.0 0.0 copy-done.4
  69.0 0.1 collective-permute-start
  69.1 1.7 collective-permute-start.2
  70.8 7.0 %collective-permute-done = bf16[192,768]{1,0:T(8,128)(2,1)S(1)} collective-permute-done((bf16[192,768]{1,0:T(8,128)(2,1)S(1)}, bf16[192,768]{1,0:T(8,128)(2,1)S(1)}, u32[]{:S(2)}, u32[]{:S(2)}) %collective-permute-start) | collective-permute-done | bytes 294944 | tf_op jit(solution)/shard_map/ppermute | solution.py:28
  77.9 0.0 collective-permute-start.1
  77.9 1.9 %collective-permute-done.2 = bf16[192,768]{1,0:T(8,128)(2,1)S(1)} collective-permute-done((bf16[192,768]{1,0:T(8,128)(2,1)S(1)}, bf16[192,768]{1,0:T(8,128)(2,1)S(1)}, u32[]{:S(2)}, u32[]{:S(2)}) %collective-permute-start.2) | collective-permute-done | bytes 294944 | tf_op jit(solution)/shard_map/ppermute | solution.py:30
  79.8 10.5 %collective-permute-done.1 = bf16[192,768]{1,0:T(8,128)(2,1)S(1)} collective-permute-done((bf16[192,768]{1,0:T(8,128)(2,1)S(1)}, bf16[192,768]{1,0:T(8,128)(2,1)S(1)}, u32[]{:S(2)}, u32[]{:S(2)}) %collective-permute-start.1) | collective-permute-done | bytes 294944 | tf_op jit(solution)/shard_map/ppermute | solution.py:28
  90.3 0.1 pad_maximum_fusion
  90.5 0.6 gather_fusion
  91.1 4.6 %all-gather.2.cloned.1.call-done = f32[768,768]{0,1:T(8,128)} async-done(((f32[768,192]{0,1:T(8,128)}), f32[768,768]{0,1:T(8,128)}) %all-gather.2.cloned.1.call-update) | async-done | bytes 2359312 | tf_op jit(solution)/shard_map/all_gather | solution.py:58
  95.7 0.0 copy-done
  95.7 3.1 %fusion.10 = f32[768,192]{0,1:T(8,128)S(1)} fusion(f32[768,768]{0,1:T(8,128)} %all-gather.2.cloned.1.call-done, bf16[1,192,768]{2,1,0:T(8,128)(2,1)S(1)} %copy-done), kind=kOutput, calls=%fused_computation.18 | convolution fusion | flops 1358954496 | bytes 3244032 | tf_op jit(solution)/shard_map/dot_general | solution.py:68
  98.9 0.9 convolution_bitcast_fusion
  99.7 0.6 copy.32
  100.3 14.1 %all_to_all.30 = f32[1,192,768]{1,0,2:T(1,128)S(1)} all-to-all(f32[1,192,768]{1,0,2:T(1,128)S(1)} %copy.32), channel_id=1, replica_groups=mesh['shard'=8,'tensor'=4] {'tensor'}, dimensions={2} | all-to-all | bytes 1179648 | tf_op jit(solution)/shard_map/all_to_all | solution.py:70
  114.4 0.4 copy.33
  114.8 0.6 all_to_all.23
  115.4 1.0 copy.34
  116.4 0.0 copy-start.6
  116.5 0.0 copy-start.7
  116.5 0.0 copy-start.8
  116.5 0.0 copy-start.1
  116.5 4.4 %all-to-all-start.2 = ((f32[8,96,192]{2,1,0:T(8,128)}), f32[8,96,192]{2,1,0:T(8,128)}, u32[]{:S(2)}, u32[]{:S(2)}) async-start(f32[8,96,192]{2,1,0:T(8,128)} %bitcast.49), calls=%async_computation.2 | async-start | bytes 1572864 | tf_op jit(solution)/shard_map/all_to_all | solution.py:73
  120.9 0.0 copy-done.6
  120.9 6.2 %psum.23 = f32[4,96]{1,0:T(4,128)S(1)} all-reduce(f32[4,96]{1,0:T(4,128)S(1)} %bitcast.60), channel_id=1, replica_groups=mesh['shard'=8,'tensor'=4] {'tensor'}, use_global_device_ids=true, to_apply=%region_5.6 | all-reduce | flops 384 | bytes 3072 | tf_op jit(solution)/shard_map/psum | solution.py:49
  127.1 0.0 copy-done.7
  127.1 0.0 copy-done.8
  127.1 0.6 add_divide_fusion
  127.7 2.1 %multiply_reduce_fusion.1 = (f32[4]{0:T(128)S(1)}, f32[4,96,192]{2,1,0:T(8,128)}) fusion(f32[4,96,192]{2,1,0:T(8,128)} %copy-done.2, f32[4,96,192]{2,1,0:T(8,128)} %param.11), kind=kLoop, calls=%fused_computation.17 | loop fusion | flops 663548 | bytes 884752 | tf_op jit(solution)/shard_map/reduce_sum | solution.py:48
  129.8 0.0 copy-done.1
  129.8 0.0 copy-start.3
  129.8 4.0 %fusion.3 = f32[1,192,768]{2,1,0:T(8,128)} fusion(f32[768,768]{0,1:T(8,128)S(1)} %copy-done.1, s32[]{:T(128)S(6)} %select_n.29, f32[1,192,768]{2,1,0:T(8,128)} %param.12), kind=kOutput, calls=%fused_computation.6 | convolution fusion | flops 1359396864 | bytes 4325380 | tf_op jit(solution)/shard_map/dot_general | solution.py:61
  133.9 0.0 copy-done.3
  133.9 4.8 %fusion.1 = f32[1,192,768]{2,1,0:T(8,128)} fusion(f32[768,192]{1,0:T(8,128)S(1)} %bitcast.46, f32[768,768]{0,1:T(8,128)S(1)} %copy-done.1, f32[1,192,768]{2,1,0:T(8,128)S(1)} %copy-done.3), kind=kOutput, calls=%fused_computation.3 | convolution fusion | flops 1359396864 | bytes 4128768 | tf_op jit(solution)/shard_map/dot_general | solution.py:64
  138.6 2.4 %all-to-all-done.2 = f32[8,96,192]{2,1,0:T(8,128)} async-done(((f32[8,96,192]{2,1,0:T(8,128)}), f32[8,96,192]{2,1,0:T(8,128)}, u32[]{:S(2)}, u32[]{:S(2)}) %all-to-all-start.2) | async-done | bytes 589856 | tf_op jit(solution)/shard_map/all_to_all | solution.py:73
  141.0 1.4 reshape.89
  142.4 0.3 dot_general.32
  142.8 1.1 multiply_reduce_fusion
  143.9 38.0 %all-reduce = (f32[4]{0:T(128)S(1)}, f32[4]{0:T(128)S(1)}) all-reduce(f32[4]{0:T(128)S(1)} %get-tuple-element.42, f32[4]{0:T(128)S(1)} %get-tuple-element.40), channel_id=1, replica_groups=mesh['shard'=8,'tensor'=4] {'shard','tensor'}, use_global_device_ids=true, to_apply=%region_4.5 | all-reduce | flops 8 | bytes 64 | tf_op jit(solution)/shard_map/psum | solution.py:83
  181.9 0.1 broadcast_multiply_fusion
  182.1 0.8 copy.36
  (3 shorter events, 0.0 us)
Async XLA Ops:
  7.2 88.6 %copy-start = (bf16[1,192,768]{2,1,0:T(8,128)(2,1)S(1)}, bf16[1,192,768]{2,1,0:T(8,128)(2,1)}, u32[]{:S(2)}) copy-start(bf16[1,192,768]{2,1,0:T(8,128)(2,1)} %param.14) | copy-start | bytes 884740
  7.2 32.2 %reduce-scatter.4.cloned.1.call-start = ((), (), s32[]{:S(2)}) async-start(), calls=%async_computation.5 | async-start | bytes 1474560
  10.8 84.9 %all-gather.2.cloned.1.call-start = ((), (), s32[]{:S(2)}) async-start(), calls=%async_computation.4 | async-start | bytes 2949120 | tf_op jit(solution)/shard_map/all_gather | solution.py:58
  40.6 0.7 copy-start.5
  40.9 1.3 copy-start.2
  67.9 1.1 copy-start.4
  69.0 8.8 %collective-permute-start = (bf16[192,768]{1,0:T(8,128)(2,1)S(1)}, bf16[192,768]{1,0:T(8,128)(2,1)S(1)}, u32[]{:S(2)}, u32[]{:S(2)}) collective-permute-start(bf16[192,768]{1,0:T(8,128)(2,1)S(1)} %bitcast.55), channel_id=1, source_target_pairs={{0,1},{1,2},{2,3},{3,0},{4,5},{5,6},{6,7},{7,4},{8,9},{9,10},{10,1... | collective-permute-start | bytes 884744 | tf_op jit(solution)/shard_map/ppermute | solution.py:28
  69.1 10.7 %collective-permute-start.2 = (bf16[192,768]{1,0:T(8,128)(2,1)S(1)}, bf16[192,768]{1,0:T(8,128)(2,1)S(1)}, u32[]{:S(2)}, u32[]{:S(2)}) collective-permute-start(bf16[192,768]{1,0:T(8,128)(2,1)S(1)} %bitcast.56), channel_id=1, source_target_pairs={{1,0},{2,1},{3,2},{0,3},{5,4},{6,5},{7,6},{4,7},{9,8},{10,9},{11,1... | collective-permute-start | bytes 884744 | tf_op jit(solution)/shard_map/ppermute | solution.py:30
  77.9 12.4 %collective-permute-start.1 = (bf16[192,768]{1,0:T(8,128)(2,1)S(1)}, bf16[192,768]{1,0:T(8,128)(2,1)S(1)}, u32[]{:S(2)}, u32[]{:S(2)}) collective-permute-start(bf16[192,768]{1,0:T(8,128)(2,1)S(1)} %collective-permute-done), channel_id=1, source_target_pairs={{0,1},{1,2},{2,3},{3,0},{4,5},{5,6},{6,7},{7,4},{8,9},{9,10},{10,1... | collective-permute-start | bytes 884744 | tf_op jit(solution)/shard_map/ppermute | solution.py:28
  116.4 4.4 %copy-start.6 = (f32[1,4,96]{2,1,0:T(4,128)S(1)}, f32[1,4,96]{2,1,0:T(4,128)}, u32[]{:S(2)}) copy-start(f32[1,4,96]{2,1,0:T(4,128)} %param.17) | copy-start | bytes 4612
  116.5 10.7 %copy-start.7 = (f32[4,96]{1,0:T(4,128)S(1)}, f32[4,96]{1,0:T(4,128)}, u32[]{:S(2)}) copy-start(f32[4,96]{1,0:T(4,128)} %param.19) | copy-start | bytes 4612
  116.5 10.7 %copy-start.8 = (f32[4,96]{1,0:T(4,128)S(1)}, f32[4,96]{1,0:T(4,128)}, u32[]{:S(2)}) copy-start(f32[4,96]{1,0:T(4,128)} %param.18) | copy-start | bytes 4612
  116.5 13.4 %copy-start.1 = (f32[768,768]{0,1:T(8,128)S(1)}, f32[768,768]{0,1:T(8,128)}, u32[]{:S(2)}) copy-start(f32[768,768]{0,1:T(8,128)} %all-gather.2.cloned.1.call-done) | copy-start | bytes 7077892
  116.5 24.5 %all-to-all-start.2 = ((f32[8,96,192]{2,1,0:T(8,128)}), f32[8,96,192]{2,1,0:T(8,128)}, u32[]{:S(2)}, u32[]{:S(2)}) async-start(f32[8,96,192]{2,1,0:T(8,128)} %bitcast.49), calls=%async_computation.2 | async-start | bytes 1572864 | tf_op jit(solution)/shard_map/all_to_all | solution.py:73
  129.8 4.0 %copy-start.3 = (f32[1,192,768]{2,1,0:T(8,128)S(1)}, f32[1,192,768]{2,1,0:T(8,128)}, u32[]{:S(2)}) copy-start(f32[1,192,768]{2,1,0:T(8,128)} %param.13) | copy-start | bytes 1769476
Sparse Core Ops, SparseCore 0:
  10.9 28.4 reduce-scatter.3
  69.1 26.5 all-gather.1
